TPU v7x, 256 devices: a whole 4x4x8 slice. The times are simulated.
256 devices in a mesh: group: 8 (over x, core), expert: 32 (over y, z).
Axes of the slice: x: 4, y: 4, z: 8, core: 2. Of those that a mesh axis runs over, the one named last changes fastest.
Arguments:
- resid: bfloat16 [32768, 2048], P(('group', 'expert')), may hold values from -6 to 6
- queries: bfloat16 [32768, 2048], P(('group', 'expert')), may hold values from -48 to 48
- span_kv: bfloat16 [2, 32768, 2048], P(None, ('group', 'expert')), may hold values from -4 to 4
- cache_kv: bfloat16 [2, 256, 2, 128, 2048], P(None, ('group', 'expert')), may hold values from -6 to 6
- seg_len: int32 [256, 2], P(('group', 'expert')), may hold values from 0 to 128, as said below
- o_rows: bfloat16 [2048, 2048], P('expert'), may hold values from -0.125 to 0.125
- norm_gain: float32 [2048], replicated, may hold values from 0.25 to 1.75
- routes: int32 [32768, 8], P(('group', 'expert')), may hold values from 0 to 31, all different within a row; in each aligned block of 128 rows (0 to 127, 128 to 255, ...) at most 48 rows name the same one
- route_wts: float32 [32768, 8], P(('group', 'expert')), may hold values from 0.05 to 0.6
- w_in: bfloat16 [32, 2048, 1024], P('expert'), may hold values from -0.125 to 0.125
- w_out: bfloat16 [32, 512, 2048], P('expert'), may hold values from -0.25 to 0.25
Outputs:
- layer_out: bfloat16 [32768, 2048], P(('group', 'expert'))
Inputs may be any that keep to these rules, and one draw needn't show every extreme that they name: seg_len[d, 0] is 1 to 128; seg_len[d, 1] is 0 (the paired request is short) or 1 to 128; seg_len[0, 0] and seg_len[0, 1] are 128 and seg_len[1, 1] is 0. `routes`: each row names 8 different experts; among the 128 rows of one device no expert is named more than 48 times.
All inputs are finite; a program needn't handle non-finite values.
Results may differ from a plain program's by a relative error of at most 0.0053.
Values may be sent and summed in bfloat16 or wider, within the bound.
A program may use at most 128 MiB of HBM per device.

v0:
```python
import math
import jax
import jax.numpy as jnp
from jax import lax
from jax.sharding import PartitionSpec as P

HEADS = 16
HD = 128
FF = 512
TOPK = 8


def swapped(block, axis, distance):
    count = lax.axis_size(axis)
    route = []
    for low in range(count):
        high = low | 1 << distance
        if high != low and high < count:
            route += [(low, high), (high, low)]
    return lax.ppermute(block, axis, route)


def attend(query_rows, key_rows, value_rows, valid_keys):
    q_heads = query_rows.reshape(query_rows.shape[0], HEADS, HD)
    k_heads = key_rows.reshape(key_rows.shape[0], HEADS, HD)
    v_heads = value_rows.reshape(value_rows.shape[0], HEADS, HD)
    scores = jnp.einsum("chd,shd->hcs", q_heads, k_heads, preferred_element_type=jnp.float32) * (
        1.0 / math.sqrt(HD)
    )
    scores = jnp.where(valid_keys[None, None, :], scores, -1e30)
    peak_score = jnp.max(scores, axis=-1)
    expo = jnp.where(valid_keys[None, None, :], jnp.exp(scores - peak_score[..., None]), 0.0)
    totals = jnp.sum(expo, axis=-1)
    probs_low = expo.astype(jnp.bfloat16)
    accum_out = jnp.einsum("hcs,shd->chd", probs_low, v_heads, preferred_element_type=jnp.float32)
    return (peak_score, totals, accum_out)


def merge_parts(first, second):
    peak_a, total_a, accum_a = first
    peak_b, total_b, accum_b = second
    peak_both = jnp.maximum(peak_a, peak_b)
    scale_a = jnp.exp(peak_a - peak_both).T
    scale_b = jnp.exp(peak_b - peak_both).T
    numer = accum_a * scale_a[:, :, None] + accum_b * scale_b[:, :, None]
    denom = total_a.T * scale_a + total_b.T * scale_b
    merged = numer / denom[:, :, None]
    return merged.reshape(merged.shape[0], -1).astype(jnp.bfloat16)


def expert_mlp(token_rows, weight_in, weight_out):
    joined = jnp.dot(token_rows, weight_in, preferred_element_type=jnp.float32)
    hidden = (jax.nn.silu(joined[:, :FF]) * joined[:, FF:]).astype(jnp.bfloat16)
    return jnp.dot(hidden, weight_out, preferred_element_type=jnp.float32).astype(jnp.bfloat16)


def shards(
    resid, queries, span_kv, cache_kv, seg_len, o_rows, norm_gain, routes, route_wts, w_in, w_out
):
    span_rows = queries.shape[0]
    seg_rows = cache_kv.shape[3]
    width = queries.shape[1]
    experts_here = lax.axis_size("expert")
    positions = jnp.arange(seg_rows, dtype=jnp.int32)
    keys_a = jnp.concatenate([span_kv[0], cache_kv[0, 0, 0]], axis=0)
    vals_a = jnp.concatenate([span_kv[1], cache_kv[1, 0, 0]], axis=0)
    valid_a = jnp.concatenate([jnp.ones((span_rows,), bool), positions < seg_len[0, 0]])
    part_a = attend(queries, keys_a, vals_a, valid_a)
    length_low = seg_len[0, 1:2].astype(jnp.float32).astype(jnp.bfloat16)
    fetched, fetched_len = swapped((cache_kv[:, 0, 1], length_low), "group", 0)
    valid_b = positions.astype(jnp.float32) < fetched_len[0].astype(jnp.float32)
    part_b = attend(queries, fetched[0], fetched[1], valid_b)
    attended = merge_parts(part_a, part_b)
    projected = jnp.dot(
        attended,
        lax.all_gather(o_rows, "expert", axis=0, tiled=True),
        preferred_element_type=jnp.float32,
    )
    residual = resid.astype(jnp.float32) + projected
    normed = (
        residual
        * lax.rsqrt(jnp.mean(residual * residual, axis=-1, keepdims=True) + 1e-05)
        * norm_gain
    ).astype(jnp.bfloat16)
    capacity = min(span_rows, span_rows * TOPK * 3 // (2 * experts_here))
    onehot = (
        routes[:, :, None] == jnp.arange(experts_here, dtype=jnp.int32)[None, None, :]
    ).astype(jnp.int32)
    counts = jnp.sum(onehot, axis=1)
    before = jnp.cumsum(counts, axis=0) - counts
    slot_ids = jnp.sum(onehot * before[:, None, :], axis=-1)
    flat_slot = routes * capacity + slot_ids
    placing = jnp.any(
        flat_slot[None, :, :]
        == jnp.arange(experts_here * capacity, dtype=jnp.int32)[:, None, None],
        axis=-1,
    )
    outgoing = jnp.dot(
        placing.astype(jnp.bfloat16), normed, preferred_element_type=jnp.float32
    ).astype(jnp.bfloat16)
    outgoing = outgoing.reshape(experts_here, capacity, width)
    arrived = lax.all_to_all(outgoing, "expert", split_axis=0, concat_axis=0, tiled=True)
    flat_rows = arrived.reshape(-1, width)
    output_rows = expert_mlp(flat_rows, w_in[0], w_out[0]).reshape(arrived.shape)
    returned_rows = lax.all_to_all(output_rows, "expert", split_axis=0, concat_axis=0, tiled=True)
    returned_rows = returned_rows.reshape(experts_here * capacity, width)
    expert_sum = jnp.zeros((span_rows, width), jnp.float32)
    for route_k in range(TOPK):
        picked = returned_rows[flat_slot[:, route_k]].astype(jnp.float32)
        expert_sum = expert_sum + route_wts[:, route_k, None] * picked
    return (residual + expert_sum).astype(jnp.bfloat16)


def solution(mesh):
    placed = (
        P(("group", "expert"), None),
        P(("group", "expert"), None),
        P(None, ("group", "expert"), None),
        P(None, ("group", "expert"), None, None, None),
        P(("group", "expert"), None),
        P("expert", None),
        P(),
        P(("group", "expert"), None),
        P(("group", "expert"), None),
        P("expert", None, None),
        P("expert", None, None),
    )
    return jax.shard_map(
        shards, mesh=mesh, in_specs=placed, out_specs=P(("group", "expert"), None), check_vma=False
    )
```

profile of v0, /device:TPU:33, one launch (start us, length us, event | category | flops | bytes accessed | tf_op | source)
XLA Modules:
  0.0 479.4 jit_solution(5816244615594503621)
XLA Ops:
  7.3 1.3 fusion.66
  9.2 1.6 collective-permute-start
  10.8 1.3 slice.87
  12.1 1.3 copy.55
  13.4 2.1 fusion.65
  15.5 1.3 copy.53
  16.8 1.1 copy.39
  17.9 2.3 fusion.63
  20.2 1.3 copy.54
  23.6 2.1 copy.36
  26.8 5.6 %fusion = pred[1536,128]{1,0:T(8,128)(4,1)S(1)} fusion(s32[128,8]{0,1:T(8,128)S(1)} %multiply_add_fusion), kind=kLoop, calls=%fused_computation.11 | loop fusion | flops 2949120 | bytes 200704 | tf_op jit(solution)/shard_map/reduce_or | solution.py:93
  32.4 1.9 bitcast_reduce_fusion
  34.2 1.3 copy-done.1
  37.0 1.4 fusion.64
  40.0 1.2 fusion.16
  41.2 67.1 %all-gather.2.cloned.1.call-done = bf16[2048,2048]{1,0:T(8,128)(2,1)} async-done(((bf16[64,2048]{1,0:T(8,128)(2,1)}), bf16[2048,2048]{1,0:T(8,128)(2,1)}) %all-gather.2.cloned.1.call-update) | async-done | bytes 8388624 | tf_op jit(solution)/shard_map/all_gather | solution.py:76
  108.3 4.9 %multiply_reduce_fusion = (f32[128]{0:T(128)S(1)}, f32[128,2048]{1,0:T(8,128)S(1)}) fusion(bf16[128,2048]{0,1:T(8,128)(2,1)} %bitcast.126, bf16[2048,2048]{1,0:T(8,128)(2,1)} %all-gather.2.cloned.1.call-done, bf16[128,2048]{1,0:T(8,128)(2,1)} %param.11), kind=kOutput, calls=%fused_computation.44 | convolution fusion | flops 1074790272 | bytes 10486272 | tf_op jit(solution)/shard_map/dot_general | solution.py:74
  113.2 1.9 convolution_convert_fusion.1
  115.1 145.8 %all_to_all.10 = bf16[32,48,2048]{2,1,0:T(8,128)(2,1)S(1)} all-to-all(bf16[32,48,2048]{2,1,0:T(8,128)(2,1)S(1)} %bitcast.120), channel_id=1, replica_groups=mesh['group'=8,'expert'=32] {'expert'}, dimensions={0} | all-to-all | bytes 12582912 | tf_op jit(solution)/shard_map/all_to_all | solution.py:102
  260.9 6.8 %fusion.1 = f32[1536,1024]{1,0:T(8,128)S(1)} fusion(bf16[1536,2048]{1,0:T(8,128)(2,1)S(1)} %bitcast.122, bf16[1,2048,1024]{2,1,0:T(8,128)(2,1)S(1)} %copy-done.9), kind=kOutput, calls=%fused_computation.12 | convolution fusion | flops 6442450944 | bytes 16777216 | tf_op jit(solution)/shard_map/dot_general | solution.py:52
  267.7 5.4 %convolution_convert_fusion = bf16[1536,2048]{1,0:T(8,128)(2,1)} fusion(bf16[1,512,2048]{2,1,0:T(8,128)(2,1)S(1)} %copy-done, f32[1536,1024]{1,0:T(8,128)S(1)} %fusion.1), kind=kOutput, calls=%fused_computation.8 | convolution fusion | flops 3229089792 | bytes 14680064 | tf_op jit(solution)/shard_map/dot_general | solution.py:54
  273.1 7.4 %all-to-all-start.1 = ((bf16[32,48,2048]{2,1,0:T(8,128)(2,1)}), bf16[32,48,2048]{2,1,0:T(8,128)(2,1)}, u32[]{:S(2)}, u32[]{:S(2)}) async-start(bf16[32,48,2048]{2,1,0:T(8,128)(2,1)} %bitcast.121), calls=%async_computation.1 | async-start | bytes 12582912 | tf_op jit(solution)/shard_map/all_to_all | solution.py:105
  280.6 140.9 %all-to-all-done.1 = bf16[32,48,2048]{2,1,0:T(8,128)(2,1)} async-done(((bf16[32,48,2048]{2,1,0:T(8,128)(2,1)}), bf16[32,48,2048]{2,1,0:T(8,128)(2,1)}, u32[]{:S(2)}, u32[]{:S(2)}) %all-to-all-start.1) | async-done | bytes 6291488 | tf_op jit(solution)/shard_map/all_to_all | solution.py:105
  421.5 5.8 %gather_fusion = bf16[128,2048]{1,0:T(8,128)(2,1)} fusion(bf16[1536,2048]{1,0:T(8,128)(2,1)} %bitcast.24, s32[1024]{0:T(1024)S(1)} %get-tuple-element.45), kind=kCustom, calls=%fused_computation | custom fusion | bytes 1049088 | tf_op jit(solution)/shard_map/gather | solution.py:109
  427.3 5.9 %gather_fusion.1 = bf16[128,2048]{1,0:T(8,128)(2,1)} fusion(bf16[1536,2048]{1,0:T(8,128)(2,1)} %bitcast.24, s32[1024]{0:T(1024)S(1)} %get-tuple-element.44), kind=kCustom, calls=%fused_computation.1 | custom fusion | bytes 1049088 | tf_op jit(solution)/shard_map/gather | solution.py:109
  433.2 5.9 %gather_fusion.2 = bf16[128,2048]{1,0:T(8,128)(2,1)} fusion(bf16[1536,2048]{1,0:T(8,128)(2,1)} %bitcast.24, s32[1024]{0:T(1024)S(1)} %get-tuple-element.43), kind=kCustom, calls=%fused_computation.2 | custom fusion | bytes 1049088 | tf_op jit(solution)/shard_map/gather | solution.py:109
  439.1 5.9 %gather_fusion.3 = bf16[128,2048]{1,0:T(8,128)(2,1)} fusion(bf16[1536,2048]{1,0:T(8,128)(2,1)} %bitcast.24, s32[1024]{0:T(1024)S(1)} %get-tuple-element.42), kind=kCustom, calls=%fused_computation.3 | custom fusion | bytes 1049088 | tf_op jit(solution)/shard_map/gather | solution.py:109
  444.9 5.8 %gather_fusion.4 = bf16[128,2048]{1,0:T(8,128)(2,1)} fusion(bf16[1536,2048]{1,0:T(8,128)(2,1)} %bitcast.24, s32[1024]{0:T(1024)S(1)} %get-tuple-element.41), kind=kCustom, calls=%fused_computation.4 | custom fusion | bytes 1049088 | tf_op jit(solution)/shard_map/gather | solution.py:109
  450.7 5.8 %gather_fusion.5 = bf16[128,2048]{1,0:T(8,128)(2,1)} fusion(bf16[1536,2048]{1,0:T(8,128)(2,1)} %bitcast.24, s32[1024]{0:T(1024)S(1)} %get-tuple-element.40), kind=kCustom, calls=%fused_computation.5 | custom fusion | bytes 1049088 | tf_op jit(solution)/shard_map/gather | solution.py:109
  456.6 6.1 %gather_fusion.6 = bf16[128,2048]{1,0:T(8,128)(2,1)} fusion(bf16[1536,2048]{1,0:T(8,128)(2,1)} %bitcast.24, s32[1024]{0:T(1024)S(1)} %get-tuple-element.39), kind=kCustom, calls=%fused_computation.6 | custom fusion | bytes 1049088 | tf_op jit(solution)/shard_map/gather | solution.py:109
  462.6 5.8 %gather_fusion.7 = bf16[128,2048]{1,0:T(8,128)(2,1)} fusion(bf16[1536,2048]{1,0:T(8,128)(2,1)} %bitcast.24, s32[1024]{0:T(1024)S(1)} %get-tuple-element.38), kind=kCustom, calls=%fused_computation.7 | custom fusion | bytes 1049088 | tf_op jit(solution)/shard_map/gather | solution.py:109
  468.5 3.9 add_convert_fusion
  (48 shorter events, 6.1 us)
Async XLA Ops:
  6.5 261.2 %copy-start = (bf16[1,512,2048]{2,1,0:T(8,128)(2,1)S(1)}, bf16[1,512,2048]{2,1,0:T(8,128)(2,1)}, u32[]{:S(2)}) copy-start(bf16[1,512,2048]{2,1,0:T(8,128)(2,1)} %param.21) | copy-start | bytes 6291460
  6.5 101.7 %all-gather.2.cloned.1.call-start = ((), (), s32[]{:S(2)}) async-start(), calls=%async_computation.2 | async-start | bytes 8650752 | tf_op jit(solution)/shard_map/all_gather | solution.py:76
  9.2 27.0 %collective-permute-start = (bf16[1]{0:T(256)(128)(2,1)}, bf16[1]{0:T(256)(128)(2,1)}, u32[]{:S(2)}, u32[]{:S(2)}) collective-permute-start(bf16[1]{0:T(256)(128)(2,1)} %bitcast.8), channel_id=1, source_target_pairs={{0,32},{32,0},{64,96},{96,64},{128,160},{160,128},{192,224},{224,1... | collective-permute-start | bytes 14 | tf_op jit(solution)/shard_map/ppermute | solution.py:20
  13.4 23.5 %collective-permute-start.1 = (bf16[2,128,2048]{1,2,0:T(8,128)(2,1)}, bf16[2,128,2048]{1,2,0:T(8,128)(2,1)}, u32[]{:S(2)}, u32[]{:S(2)}) collective-permute-start(bf16[2,128,2048]{1,2,0:T(8,128)(2,1)} %bitcast.127), channel_id=1, source_target_pairs={{0,32},{32,0},{64,96},{96,64},{128,160},{160,128},{192,224},{224,1... | collective-permute-start | bytes 3145736 | tf_op jit(solution)/shard_map/ppermute | solution.py:20
  17.9 7.8 %copy-start.6 = (s32[128,8]{0,1:T(8,128)S(1)}, s32[128,8]{0,1:T(8,128)}, u32[]{:S(2)}) copy-start(s32[128,8]{0,1:T(8,128)} %param.18) | copy-start | bytes 12292
  34.2 1.4 copy-start.1
  34.2 4.2 copy-start.3
  36.2 3.0 copy-start.4
  36.9 2.3 copy-start.2
  36.9 2.3 copy-start.5
  108.3 5.0 %copy-start.7 = (f32[2048]{0:T(1024)S(1)}, f32[2048]{0:T(1024)}, u32[]{:S(2)}) copy-start(f32[2048]{0:T(1024)} %param.17) | copy-start | bytes 24580
  115.1 145.8 %copy-start.9 = (bf16[1,2048,1024]{2,1,0:T(8,128)(2,1)S(1)}, bf16[1,2048,1024]{2,1,0:T(8,128)(2,1)}, u32[]{:S(2)}) copy-start(bf16[1,2048,1024]{2,1,0:T(8,128)(2,1)} %param.20) | copy-start | bytes 12582916
  273.1 7.4 %copy-start.8 = (f32[128,8]{0,1:T(8,128)S(1)}, f32[128,8]{0,1:T(8,128)}, u32[]{:S(2)}) copy-start(f32[128,8]{0,1:T(8,128)} %param.19) | copy-start | bytes 12292
  273.1 148.4 %all-to-all-start.1 = ((bf16[32,48,2048]{2,1,0:T(8,128)(2,1)}), bf16[32,48,2048]{2,1,0:T(8,128)(2,1)}, u32[]{:S(2)}, u32[]{:S(2)}) async-start(bf16[32,48,2048]{2,1,0:T(8,128)(2,1)} %bitcast.121), calls=%async_computation.1 | async-start | bytes 12582912 | tf_op jit(solution)/shard_map/all_to_all | solution.py:105
Sparse Core Ops, SparseCore 0:
  9.9 98.2 all-gather.1
where the time goes:
time: 489 us; the launch traced here: 479 us
  waiting for transfers between devices  209 us (43%)
  blocking collectives  146 us (30%)
  local copies, waits for them, and re-layouts  66.1 us (14%)
  matrix products  23.3 us (5%)
  between operations  15.3 us (3%)
  other arithmetic  11.2 us (2%)
  starting transfers between devices  8.94 us (2%)
    all_to_all x1, blocking collectives, shards(): lax.all_to_all(outgoing, 'expert', split_axis=0, concat_axis=0, tiled=True)  146 us
    all_to_all x1, waiting for transfers between devices, shards(): lax.all_to_all(output_rows, 'expert', split_axis=0, concat_axis=0, tiled=...  141 us
    all_gather x1, waiting for transfers between devices, shards(): lax.all_gather(o_rows, 'expert', axis=0, tiled=True)  67.1 us
    gather x8, local copies, waits for them, and re-layouts, shards(): picked = returned_rows[flat_slot[:, route_k]].astype(jnp.float32)  47 us
  transfers between devices with their start and end apart: 4, of which 2 were waited for; matrix products, arithmetic and copies ran while one was open for 6% of the time, Pallas kernels for 0%

commit v1 on v0

--- a/solution.py
+++ b/solution.py
@@ -73,7 +73,15 @@
     attended = merge_parts(part_a, part_b)
     projected = jnp.dot(
         attended,
-        lax.all_gather(o_rows, "expert", axis=0, tiled=True),
+        jnp.concatenate(
+            lax.all_to_all(
+                jnp.stack([o_rows for _ in range(lax.axis_size("expert"))], 0),
+                axis_name="expert",
+                split_axis=0,
+                concat_axis=0,
+            ),
+            0,
+        ),
         preferred_element_type=jnp.float32,
     )
     residual = resid.astype(jnp.float32) + projected

time: 489 us -> 576 us (1.18); the launches traced: 479 us -> 573 us
  waiting for transfers between devices: 209 us -> 298 us
  between operations: 15.3 us -> 1.98 us
  starting transfers between devices: 8.94 us -> 20.1 us
    all_to_all x0 -> x1, waiting for transfers between devices: none -> 158 us  [shards(): lax.all_to_all(jnp.stack([o_rows for _ in range(lax.axis_size('expert'))]...]
    all_gather x1 -> x0, waiting for transfers between devices: 67.1 us -> none  [shards(): lax.all_gather(o_rows, 'expert', axis=0, tiled=True)]
    all_to_all x0 -> x1, starting transfers between devices: none -> 11 us  [shards(): lax.all_to_all(jnp.stack([o_rows for _ in range(lax.axis_size('expert'))]...]
  transfers between devices with their start and end apart: 4 -> 4, of which waited for: 2 -> 2; matrix products, arithmetic and copies ran while one was open for 6% -> 5% of each run, Pallas kernels for 0% -> 0%
where the time goes in v1:
time: 576 us; the launch traced here: 573 us
  waiting for transfers between devices  298 us (52%)
  blocking collectives  148 us (26%)
  local copies, waits for them, and re-layouts  69.3 us (12%)
  matrix products  23.4 us (4%)
  starting transfers between devices  20.1 us (3%)
  other arithmetic  11.2 us (2%)
    all_to_all x1, waiting for transfers between devices, shards(): lax.all_to_all(jnp.stack([o_rows for _ in range(lax.axis_size('expert'))]...  158 us
    all_to_all x1, blocking collectives, shards(): lax.all_to_all(outgoing, 'expert', split_axis=0, concat_axis=0, tiled=True)  148 us
    all_to_all x1, waiting for transfers between devices, shards(): lax.all_to_all(output_rows, 'expert', split_axis=0, concat_axis=0, tiled=...  141 us
    gather x8, local copies, waits for them, and re-layouts, shards(): picked = returned_rows[flat_slot[:, route_k]].astype(jnp.float32)  47 us
  transfers between devices with their start and end apart: 4, of which 2 were waited for; matrix products, arithmetic and copies ran while one was open for 5% of the time, Pallas kernels for 0%

profile of v1, /device:TPU:33, one launch (start us, length us, event | category | flops | bytes accessed | tf_op | source)
XLA Modules:
  0.0 572.7 jit_solution(9070720545504948641)
XLA Ops:
  0.0 5.4 stack.2
  5.4 11.0 %all-to-all-start = ((bf16[32,64,2048]{2,1,0:T(8,128)(2,1)}), bf16[32,64,2048]{2,1,0:T(8,128)(2,1)}, u32[]{:S(2)}, u32[]{:S(2)}) async-start(bf16[32,64,2048]{2,1,0:T(8,128)(2,1)} %stack.2), calls=%async_computation | async-start | bytes 16777216 | tf_op jit(solution)/shard_map/all_to_all | solution.py:77
  17.6 2.1 collective-permute-start
  19.8 1.3 copy.55
  21.4 2.1 fusion.65
  23.5 1.3 copy.53
  24.8 1.0 copy.39
  25.8 2.3 fusion.63
  28.1 1.3 copy.54
  31.4 2.0 copy.36
  34.6 5.6 fusion
  40.1 1.8 bitcast_reduce_fusion
  42.0 1.3 copy-done.1
  44.8 1.4 fusion.64
  47.8 1.2 fusion.16
  49.0 157.6 %all-to-all-done = bf16[32,64,2048]{2,1,0:T(8,128)(2,1)} async-done(((bf16[32,64,2048]{2,1,0:T(8,128)(2,1)}), bf16[32,64,2048]{2,1,0:T(8,128)(2,1)}, u32[]{:S(2)}, u32[]{:S(2)}) %all-to-all-start) | async-done | bytes 8388640 | tf_op jit(solution)/shard_map/all_to_all | solution.py:77
  206.6 4.9 multiply_reduce_fusion
  211.6 1.9 convolution_convert_fusion.1
  213.4 148.4 %all_to_all.15 = bf16[32,48,2048]{2,1,0:T(8,128)(2,1)S(1)} all-to-all(bf16[32,48,2048]{2,1,0:T(8,128)(2,1)S(1)} %bitcast.121), channel_id=1, replica_groups=mesh['group'=8,'expert'=32] {'expert'}, dimensions={0} | all-to-all | bytes 12582912 | tf_op jit(solution)/shard_map/all_to_all | solution.py:110
  361.9 6.8 %fusion.1 = f32[1536,1024]{1,0:T(8,128)S(1)} fusion(bf16[1536,2048]{1,0:T(8,128)(2,1)S(1)} %bitcast.123, bf16[1,2048,1024]{2,1,0:T(8,128)(2,1)S(1)} %copy-done.10), kind=kOutput, calls=%fused_computation.12 | convolution fusion | flops 6442450944 | bytes 16777216 | tf_op jit(solution)/shard_map/dot_general | solution.py:52
  368.7 5.4 convolution_convert_fusion
  374.1 6.7 %all-to-all-start.2 = ((bf16[32,48,2048]{2,1,0:T(8,128)(2,1)}), bf16[32,48,2048]{2,1,0:T(8,128)(2,1)}, u32[]{:S(2)}, u32[]{:S(2)}) async-start(bf16[32,48,2048]{2,1,0:T(8,128)(2,1)} %bitcast.122), calls=%async_computation.2 | async-start | bytes 12582912 | tf_op jit(solution)/shard_map/all_to_all | solution.py:113
  380.9 140.7 %all-to-all-done.2 = bf16[32,48,2048]{2,1,0:T(8,128)(2,1)} async-done(((bf16[32,48,2048]{2,1,0:T(8,128)(2,1)}), bf16[32,48,2048]{2,1,0:T(8,128)(2,1)}, u32[]{:S(2)}, u32[]{:S(2)}) %all-to-all-start.2) | async-done | bytes 6291488 | tf_op jit(solution)/shard_map/all_to_all | solution.py:113
  521.6 5.8 %gather_fusion = bf16[128,2048]{1,0:T(8,128)(2,1)} fusion(bf16[1536,2048]{1,0:T(8,128)(2,1)} %bitcast.25, s32[1024]{0:T(1024)S(1)} %get-tuple-element.45), kind=kCustom, calls=%fused_computation | custom fusion | bytes 1049088 | tf_op jit(solution)/shard_map/gather | solution.py:117
  527.4 5.9 %gather_fusion.1 = bf16[128,2048]{1,0:T(8,128)(2,1)} fusion(bf16[1536,2048]{1,0:T(8,128)(2,1)} %bitcast.25, s32[1024]{0:T(1024)S(1)} %get-tuple-element.44), kind=kCustom, calls=%fused_computation.1 | custom fusion | bytes 1049088 | tf_op jit(solution)/shard_map/gather | solution.py:117
  533.3 5.9 %gather_fusion.2 = bf16[128,2048]{1,0:T(8,128)(2,1)} fusion(bf16[1536,2048]{1,0:T(8,128)(2,1)} %bitcast.25, s32[1024]{0:T(1024)S(1)} %get-tuple-element.43), kind=kCustom, calls=%fused_computation.2 | custom fusion | bytes 1049088 | tf_op jit(solution)/shard_map/gather | solution.py:117
  539.2 5.9 %gather_fusion.3 = bf16[128,2048]{1,0:T(8,128)(2,1)} fusion(bf16[1536,2048]{1,0:T(8,128)(2,1)} %bitcast.25, s32[1024]{0:T(1024)S(1)} %get-tuple-element.42), kind=kCustom, calls=%fused_computation.3 | custom fusion | bytes 1049088 | tf_op jit(solution)/shard_map/gather | solution.py:117
  545.0 5.8 %gather_fusion.4 = bf16[128,2048]{1,0:T(8,128)(2,1)} fusion(bf16[1536,2048]{1,0:T(8,128)(2,1)} %bitcast.25, s32[1024]{0:T(1024)S(1)} %get-tuple-element.41), kind=kCustom, calls=%fused_computation.4 | custom fusion | bytes 1049088 | tf_op jit(solution)/shard_map/gather | solution.py:117
  550.8 5.8 %gather_fusion.5 = bf16[128,2048]{1,0:T(8,128)(2,1)} fusion(bf16[1536,2048]{1,0:T(8,128)(2,1)} %bitcast.25, s32[1024]{0:T(1024)S(1)} %get-tuple-element.40), kind=kCustom, calls=%fused_computation.5 | custom fusion | bytes 1049088 | tf_op jit(solution)/shard_map/gather | solution.py:117
  556.7 6.1 %gather_fusion.6 = bf16[128,2048]{1,0:T(8,128)(2,1)} fusion(bf16[1536,2048]{1,0:T(8,128)(2,1)} %bitcast.25, s32[1024]{0:T(1024)S(1)} %get-tuple-element.39), kind=kCustom, calls=%fused_computation.6 | custom fusion | bytes 1049088 | tf_op jit(solution)/shard_map/gather | solution.py:117
  562.8 5.8 %gather_fusion.7 = bf16[128,2048]{1,0:T(8,128)(2,1)} fusion(bf16[1536,2048]{1,0:T(8,128)(2,1)} %bitcast.25, s32[1024]{0:T(1024)S(1)} %get-tuple-element.38), kind=kCustom, calls=%fused_computation.7 | custom fusion | bytes 1049088 | tf_op jit(solution)/shard_map/gather | solution.py:117
  568.6 3.9 add_convert_fusion
  (51 shorter events, 6.2 us)
Async XLA Ops:
  0.0 368.7 %copy-start = (bf16[1,512,2048]{2,1,0:T(8,128)(2,1)S(1)}, bf16[1,512,2048]{2,1,0:T(8,128)(2,1)}, u32[]{:S(2)}) copy-start(bf16[1,512,2048]{2,1,0:T(8,128)(2,1)} %param.21) | copy-start | bytes 6291460
  5.4 11.0 %copy-start.9 = (s32[1,2]{1,0:T(1,128)S(1)}, s32[1,2]{1,0:T(1,128)}, u32[]{:S(2)}) copy-start(s32[1,2]{1,0:T(1,128)} %param.15) | copy-start | bytes 28
  5.4 14.4 %slice-start = ((bf16[2,1,2,128,2048]{4,3,2,1,0:T(8,128)(2,1)}), bf16[2,1,1,128,2048]{4,3,2,1,0:T(8,128)(2,1)S(1)}, s32[]{:S(2)}) async-start(bf16[2,1,2,128,2048]{4,3,2,1,0:T(8,128)(2,1)} %param.14), calls=%async_computation.3 | async-start | bytes 2097152 | tf_op jit(solution)/shard_map/slice | solution.py:70
  5.4 201.2 %all-to-all-start = ((bf16[32,64,2048]{2,1,0:T(8,128)(2,1)}), bf16[32,64,2048]{2,1,0:T(8,128)(2,1)}, u32[]{:S(2)}, u32[]{:S(2)}) async-start(bf16[32,64,2048]{2,1,0:T(8,128)(2,1)} %stack.2), calls=%async_computation | async-start | bytes 16777216 | tf_op jit(solution)/shard_map/all_to_all | solution.py:77
  17.6 26.4 %collective-permute-start = (bf16[1]{0:T(256)(128)(2,1)}, bf16[1]{0:T(256)(128)(2,1)}, u32[]{:S(2)}, u32[]{:S(2)}) collective-permute-start(bf16[1]{0:T(256)(128)(2,1)} %bitcast.8), channel_id=1, source_target_pairs={{0,32},{32,0},{64,96},{96,64},{128,160},{160,128},{192,224},{224,1... | collective-permute-start | bytes 14 | tf_op jit(solution)/shard_map/ppermute | solution.py:20
  21.1 23.7 %collective-permute-start.1 = (bf16[2,128,2048]{1,2,0:T(8,128)(2,1)}, bf16[2,128,2048]{1,2,0:T(8,128)(2,1)}, u32[]{:S(2)}, u32[]{:S(2)}) collective-permute-start(bf16[2,128,2048]{1,2,0:T(8,128)(2,1)} %bitcast.128), channel_id=1, source_target_pairs={{0,32},{32,0},{64,96},{96,64},{128,160},{160,128},{192,224},{224,1... | collective-permute-start | bytes 3145736 | tf_op jit(solution)/shard_map/ppermute | solution.py:20
  25.8 7.7 %copy-start.6 = (s32[128,8]{0,1:T(8,128)S(1)}, s32[128,8]{0,1:T(8,128)}, u32[]{:S(2)}) copy-start(s32[128,8]{0,1:T(8,128)} %param.18) | copy-start | bytes 12292
  42.0 1.4 copy-start.1
  42.0 4.2 copy-start.3
  44.0 3.0 copy-start.4
  44.8 2.3 copy-start.2
  44.8 2.3 copy-start.5
  206.6 5.0 copy-start.7
  213.4 148.5 %copy-start.10 = (bf16[1,2048,1024]{2,1,0:T(8,128)(2,1)S(1)}, bf16[1,2048,1024]{2,1,0:T(8,128)(2,1)}, u32[]{:S(2)}) copy-start(bf16[1,2048,1024]{2,1,0:T(8,128)(2,1)} %param.20) | copy-start | bytes 12582916
  374.1 6.8 %copy-start.8 = (f32[128,8]{0,1:T(8,128)S(1)}, f32[128,8]{0,1:T(8,128)}, u32[]{:S(2)}) copy-start(f32[128,8]{0,1:T(8,128)} %param.19) | copy-start | bytes 12292
  374.1 147.5 %all-to-all-start.2 = ((bf16[32,48,2048]{2,1,0:T(8,128)(2,1)}), bf16[32,48,2048]{2,1,0:T(8,128)(2,1)}, u32[]{:S(2)}, u32[]{:S(2)}) async-start(bf16[32,48,2048]{2,1,0:T(8,128)(2,1)} %bitcast.122), calls=%async_computation.2 | async-start | bytes 12582912 | tf_op jit(solution)/shard_map/all_to_all | solution.py:113
